TPU v7x, 32 devices: a whole 2x2x4 slice. The times are simulated.
32 devices in a mesh: dp: 8 (over z, y), tensor: 4 (over x, core).
Axes of the slice: x: 2, y: 2, z: 4, core: 2. Of those that a mesh axis runs over, the one named last changes fastest.
Arguments:
- hidden: bfloat16 [128, 4608], P('dp'), may hold values from -6 to 6
- tied_table: bfloat16 [16384, 4608], P(('dp', 'tensor')), may hold values from -0.25 to 0.25
- targets: int32 [128], P('dp'), may hold values from 0 to 16383
- loss_weight: bfloat16 [128], P('dp'), may hold values from 2 to 20
- inputs: int32 [128], P('dp'), may hold values from 0 to 16383
- embed_grad: bfloat16 [128, 4608], P('dp'), may hold values from -0.09375 to 0.09375
Outputs:
- table_grad: bfloat16 [16384, 4608], P(('dp', 'tensor'))
- hidden_grad: float32 [128, 4608], P('dp', 'tensor')
All inputs are finite; a program needn't handle non-finite values.
Results may differ from a plain program's by a relative error of at most 0.0052.
Values may be sent and summed in bfloat16 or wider, within the bound.
A program may use at most 64 MiB of HBM per device.

v0:
```python
import math
import jax
import jax.numpy as jnp
from jax import lax
from jax.sharding import PartitionSpec as P


def squashed(hidden_rows, tied_table):
    logits = lax.dot_general(
        hidden_rows, tied_table, (((1,), (1,)), ((), ())), preferred_element_type=jnp.float32
    )
    return jnp.tanh(logits / 30.0)


def per_device(hidden, tied_table, targets, loss_weight, inputs, embed_grad):
    width = hidden.shape[1]
    vocab_rows = tied_table.shape[0]
    hidden_all, grad_all, target_all, weight_all, input_all = (
        lax.all_gather(hidden, "dp", axis=0, tiled=True),
        lax.all_gather(embed_grad, "dp", axis=0, tiled=True),
        lax.all_gather(targets, "dp", axis=0, tiled=True),
        lax.all_gather(loss_weight, "dp", axis=0, tiled=True),
        lax.all_gather(inputs, "dp", axis=0, tiled=True),
    )
    offset = lax.axis_index(("dp", "tensor")) * vocab_rows
    columns = offset + jnp.arange(vocab_rows)
    squash = squashed(hidden_all, tied_table)
    expo = jnp.exp(30.0 * squash)
    total = lax.psum(jnp.sum(expo, axis=1), ("dp", "tensor"))
    hits = (target_all[:, None] == columns[None, :]).astype(jnp.float32)
    weights = weight_all.astype(jnp.float32)
    dlogit = (weights[:, None] * (expo / total[:, None] - hits) * (1.0 - squash * squash)).astype(
        jnp.bfloat16
    )
    group_rows = lax.psum_scatter(
        jnp.dot(dlogit, tied_table, preferred_element_type=jnp.float32),
        "dp",
        scatter_dimension=0,
        tiled=True,
    )
    hidden_grad = lax.psum_scatter(group_rows, "tensor", scatter_dimension=1, tiled=True)
    head_term = lax.dot_general(
        dlogit, hidden_all, (((0,), (0,)), ((), ())), preferred_element_type=jnp.float32
    )
    onehot = (input_all[None, :] == columns[:, None]).astype(jnp.bfloat16)
    embed_term = jnp.dot(onehot, grad_all, preferred_element_type=jnp.float32)
    table_grad = (head_term + math.sqrt(width) * embed_term).astype(jnp.bfloat16)
    return (table_grad, hidden_grad)


def solution(mesh):
    placed = (P("dp", None), P(("dp", "tensor"), None), P("dp"), P("dp"), P("dp"), P("dp", None))
    return jax.shard_map(
        per_device,
        mesh=mesh,
        in_specs=placed,
        out_specs=(P(("dp", "tensor"), None), P("dp", "tensor")),
        check_vma=False,
    )
```

profile of v0, /device:TPU:0, one launch (start us, length us, event | category | flops | bytes accessed | tf_op | source)
XLA Modules:
  0.0 241.8 jit_solution(12632579317556245795)
XLA Ops:
  7.2 0.0 all-gather.3.cloned.1.call-start
  7.2 0.7 all-gather.3.cloned.1.call-update
  7.9 0.0 reduce-scatter.3.cloned.1.call-start
  8.0 1.2 dynamic-slice
  9.9 0.9 dynamic-update-slice
  10.7 23.2 %all-reduce = bf16[128]{0:T(256)(128)(2,1)S(1)} all-reduce(bf16[128]{0:T(256)(128)(2,1)S(1)} %dynamic-update-slice), channel_id=1, replica_groups=mesh['dp'=8,'tensor'=4] {'dp'}, use_global_device_ids=true, to_apply=%add | all-reduce | flops 128 | bytes 512
  34.0 0.9 dynamic-update-slice.1
  34.8 0.8 dynamic-update-slice.2
  35.7 6.8 %all-reduce.3 = (s32[128]{0:T(128)S(1)}, s32[128]{0:T(128)S(1)}) all-reduce(s32[128]{0:T(128)S(1)} %dynamic-update-slice.1, s32[128]{0:T(128)S(1)} %dynamic-update-slice.2), channel_id=1, replica_groups=mesh['dp'=8,'tensor'=4] {'dp'}, use_global_device_ids=true, to_apply=%add.1 | all-reduce | flops 256 | bytes 2048
  42.5 11.3 %all-gather.3.cloned.1.call-done = bf16[128,4608]{1,0:T(8,128)(2,1)} async-done(((bf16[16,4608]{1,0:T(8,128)(2,1)}), bf16[128,4608]{1,0:T(8,128)(2,1)}) %all-gather.3.cloned.1.call-update) | async-done | bytes 1179664 | tf_op jit(solution)/shard_map/all_gather | solution.py:19
  53.8 4.4 %fusion.1 = (f32[128]{0:T(128)S(1)}, f32[128,512]{1,0:T(8,128)S(1)}) fusion(bf16[128,4608]{1,0:T(8,128)(2,1)} %all-gather.3.cloned.1.call-done, bf16[512,4608]{1,0:T(8,128)(2,1)} %param.7), kind=kOutput, calls=%fused_computation.5 | convolution fusion | flops 604176256 | bytes 6160896 | tf_op jit(solution)/shard_map/dot_general | solution.py:9
  58.3 38.7 %psum.7 = f32[128]{0:T(128)S(1)} all-reduce(f32[128]{0:T(128)S(1)} %get-tuple-element.4), channel_id=1, replica_groups=mesh['dp'=8,'tensor'=4] {'dp','tensor'}, use_global_device_ids=true, to_apply=%region_1.0 | all-reduce | flops 128 | bytes 1024 | tf_op jit(solution)/shard_map/psum | solution.py:29
  96.9 0.0 copy-start
  96.9 4.7 %fusion.5 = f32[128,4608]{1,0:T(8,128)} fusion(bf16[512,4608]{1,0:T(8,128)(2,1)} %param.7, f32[128,512]{1,0:T(8,128)S(1)} %get-tuple-element.5, s32[512]{0:T(512)S(1)} %iota_add_fusion, f32[128]{0:T(128)S(1)} %psum.7, f32[128]{0:T(128)S(1)} %convert_element_type.13, s32[128]{0:T(128)S(1)} %get-tuple-element.2), kind=kOutput, calls=%fused_computation.10 | convolution fusion | flops 604635136 | bytes 7343616 | tf_op jit(solution)/shard_map/dot_general | solution.py:36
  101.6 0.0 reduce-scatter.3.cloned.1.call-update
  101.7 0.0 all-gather.5.cloned.1.call-start
  101.7 0.7 all-gather.5.cloned.1.call-update
  102.4 0.0 reduce-scatter.5.cloned.1.call-start
  102.5 0.0 copy-done
  102.5 5.2 %fusion.6 = f32[512,4608]{1,0:T(8,128)} fusion(bf16[128,4608]{1,0:T(8,128)(2,1)S(1)} %copy-done, f32[128,512]{1,0:T(8,128)S(1)} %get-tuple-element.5, s32[512]{0:T(512)S(1)} %iota_add_fusion, f32[128]{0:T(128)S(1)} %psum.7, f32[128]{0:T(128)S(1)} %convert_element_type.13, s32[128]{0:T(128)S(1)} %get-tuple-element.2), kind=kOutput, calls=%fused_computation.11 | convolution fusion | flops 604635136 | bytes 10882560 | tf_op jit(solution)/shard_map/dot_general | solution.py:42
  107.6 63.3 %reduce-scatter.3.cloned.1.call-done = f32[16,4608]{1,0:T(8,128)} async-done(((f32[128,4608]{1,0:T(8,128)}), f32[16,4608]{1,0:T(8,128)}) %reduce-scatter.3.cloned.1.call-update) | async-done | bytes 294928 | tf_op jit(solution)/shard_map/reduce_scatter | solution.py:35
  171.0 0.0 reduce-scatter.5.cloned.1.call-update
  171.0 42.3 %all-gather.5.cloned.1.call-done = bf16[128,4608]{1,0:T(8,128)(2,1)} async-done(((bf16[16,4608]{1,0:T(8,128)(2,1)}), bf16[128,4608]{1,0:T(8,128)(2,1)}) %all-gather.5.cloned.1.call-update) | async-done | bytes 1179664 | tf_op jit(solution)/shard_map/all_gather | solution.py:20
  213.3 7.7 %add_convert_fusion = bf16[512,4608]{1,0:T(8,128)(2,1)} fusion(f32[512,4608]{1,0:T(8,128)} %fusion.6, bf16[128,4608]{1,0:T(8,128)(2,1)} %all-gather.5.cloned.1.call-done, s32[128]{0:T(128)S(1)} %get-tuple-element.3, s32[512]{0:T(512)S(1)} %iota_add_fusion), kind=kOutput, calls=%fused_computation | convolution fusion | flops 611123200 | bytes 15337984 | tf_op jit(solution)/shard_map/dot_general | solution.py:46
  220.9 14.3 %reduce-scatter.5.cloned.1.call-done = f32[16,1152]{1,0:T(8,128)} async-done(((f32[16,4608]{1,0:T(8,128)}), f32[16,1152]{1,0:T(8,128)}) %reduce-scatter.5.cloned.1.call-update) | async-done | bytes 73744 | tf_op jit(solution)/shard_map/reduce_scatter | solution.py:41
  (5 shorter events, 0.0 us)
Async XLA Ops:
  7.2 46.7 %all-gather.3.cloned.1.call-start = ((), (), s32[]{:S(2)}) async-start(), calls=%async_computation.2 | async-start | bytes 1327104 | tf_op jit(solution)/shard_map/all_gather | solution.py:19
  7.9 163.1 %reduce-scatter.3.cloned.1.call-start = ((), (), s32[]{:S(2)}) async-start(), calls=%async_computation.4 | async-start | bytes 2654208 | tf_op jit(solution)/shard_map/reduce_scatter | solution.py:35
  96.9 5.5 %copy-start = (bf16[128,4608]{1,0:T(8,128)(2,1)S(1)}, bf16[128,4608]{1,0:T(8,128)(2,1)}, u32[]{:S(2)}) copy-start(bf16[128,4608]{1,0:T(8,128)(2,1)} %all-gather.3.cloned.1.call-done) | copy-start | bytes 3538948
  101.7 111.6 %all-gather.5.cloned.1.call-start = ((), (), s32[]{:S(2)}) async-start(), calls=%async_computation.3 | async-start | bytes 1327104 | tf_op jit(solution)/shard_map/all_gather | solution.py:20
  102.4 132.9 %reduce-scatter.5.cloned.1.call-start = ((), (), s32[]{:S(2)}) async-start(), calls=%async_computation.5 | async-start | bytes 368640 | tf_op jit(solution)/shard_map/reduce_scatter | solution.py:41
Sparse Core Ops, SparseCore 0:
  10.2 43.6 all-gather.2
  101.8 69.1 reduce-scatter.2
  173.1 40.0 all-gather.4
  216.2 19.0 reduce-scatter.4
where the time goes:
time: 242 us
  waiting for transfers between devices  133 us (55%)
  blocking collectives  68.7 us (28%)
  matrix products  22 us (9%)
  between operations  14.5 us (6%)
  local copies, waits for them, and re-layouts  3.81 us (2%)
    reduce_scatter x1, waiting for transfers between devices, per_device(): lax.psum_scatter(jnp.dot(dlogit, tied_table, preferred_element_type=jnp.f...  63.3 us
    all_gather x1, waiting for transfers between devices, per_device(): lax.all_gather(embed_grad, 'dp', axis=0, tiled=True)  42.3 us
    psum x1, blocking collectives, per_device(): total = lax.psum(jnp.sum(expo, axis=1), ('dp', 'tensor'))  38.7 us
    unnamed x2, blocking collectives  30.1 us
    reduce_scatter x1, waiting for transfers between devices, per_device(): lax.psum_scatter(group_rows, 'tensor', scatter_dimension=1, tiled=True)  14.3 us
    all_gather x1, waiting for transfers between devices, per_device(): lax.all_gather(hidden, 'dp', axis=0, tiled=True)  11.3 us
    dot_general x1, matrix products, per_device(): embed_term = jnp.dot(onehot, grad_all, preferred_element_type=jnp.float32)  7.67 us
    dot_general x1, matrix products, per_device(): lax.dot_general(dlogit, hidden_all, (((0,), (0,)), ((), ())), preferred_e...  5.16 us
  transfers between devices with their start and end apart: 4, of which 4 were waited for; matrix products, arithmetic and copies ran while one was open for 7% of the time, Pallas kernels for 0%

commit v1 on v0

--- a/solution.py
+++ b/solution.py
@@ -3,6 +3,19 @@
 import jax.numpy as jnp
 from jax import lax
 from jax.sharding import PartitionSpec as P
+
+
+def gather_around(value, axis, dim):
+    ways = lax.axis_size(axis)
+    up = [(d, (d + 1) % ways) for d in range(ways)]
+    down = [(d, (d - 1) % ways) for d in range(ways)]
+    earlier, later = ([value], [value])
+    for _ in range(ways // 2):
+        earlier.append(lax.ppermute(earlier[-1], axis, up))
+    for _ in range((ways - 1) // 2):
+        later.append(lax.ppermute(later[-1], axis, down))
+    line = jnp.concatenate([*earlier[::-1], *later[1:]], axis=dim)
+    return jnp.roll(line, (lax.axis_index(axis) - ways // 2) * value.shape[dim], axis=dim)
 
 
 def squashed(hidden_rows, tied_table):
@@ -16,7 +29,7 @@
     width = hidden.shape[1]
     vocab_rows = tied_table.shape[0]
     hidden_all, grad_all, target_all, weight_all, input_all = (
-        lax.all_gather(hidden, "dp", axis=0, tiled=True),
+        gather_around(hidden, "dp", 0),
         lax.all_gather(embed_grad, "dp", axis=0, tiled=True),
         lax.all_gather(targets, "dp", axis=0, tiled=True),
         lax.all_gather(loss_weight, "dp", axis=0, tiled=True),

time: 242 us -> 263 us (1.087)
  starting transfers between devices: 0.16 us -> 17.3 us
  waiting for transfers between devices: 133 us -> 143 us
  matrix products: 22 us -> 12.8 us
    ppermute x0 -> x7, starting transfers between devices: none -> 17.2 us  [the longest x3 13.6 us: gather_around(): later.append(lax.ppermute(later[-1], axis, down))]
    ppermute x0 -> x7, waiting for transfers between devices: none -> 15 us  [the longest x4 13.3 us: gather_around(): earlier.append(lax.ppermute(earlier[-1], axis, up))]
    all_gather x1 -> x0, waiting for transfers between devices: 11.3 us -> none  [per_device(): lax.all_gather(hidden, 'dp', axis=0, tiled=True)]
    reduce_scatter x1, waiting for transfers between devices: 63.3 us -> 68.9 us  [per_device(): lax.psum_scatter(jnp.dot(dlogit, tied_table, preferred_element_type=jnp.f...]
    dot_general x1, matrix products: 7.67 us -> 2.69 us  [per_device(): embed_term = jnp.dot(onehot, grad_all, preferred_element_type=jnp.float32)]
    dot_general x1, matrix products: 4.45 us -> 1.75 us  [squashed(): lax.dot_general(hidden_rows, tied_table, (((1,), (1,)), ((), ())), prefer...]
    unnamed x9 -> x24, local copies, waits for them, and re-layouts: 3.81 us -> 5.8 us
  transfers between devices with their start and end apart: 4 -> 10, of which waited for: 4 -> 7; matrix products, arithmetic and copies ran while one was open for 7% -> 4% of each run, Pallas kernels for 0% -> 0%
where the time goes in v1:
time: 263 us; the launch traced here: 262 us
  waiting for transfers between devices  143 us (54%)
  blocking collectives  69.2 us (26%)
  starting transfers between devices  17.3 us (7%)
  between operations  14.5 us (6%)
  matrix products  12.8 us (5%)
  local copies, waits for them, and re-layouts  5.81 us (2%)
    reduce_scatter x1, waiting for transfers between devices, per_device(): lax.psum_scatter(jnp.dot(dlogit, tied_table, preferred_element_type=jnp.f...  68.9 us
    all_gather x1, waiting for transfers between devices, per_device(): lax.all_gather(embed_grad, 'dp', axis=0, tiled=True)  42.3 us
    psum x1, blocking collectives, per_device(): total = lax.psum(jnp.sum(expo, axis=1), ('dp', 'tensor'))  40.6 us
    unnamed x2, blocking collectives  28.6 us
    reduce_scatter x1, waiting for transfers between devices, per_device(): lax.psum_scatter(group_rows, 'tensor', scatter_dimension=1, tiled=True)  15.7 us
    ppermute x3, starting transfers between devices, gather_around(): later.append(lax.ppermute(later[-1], axis, down))  13.6 us
    ppermute x4, waiting for transfers between devices, gather_around(): earlier.append(lax.ppermute(earlier[-1], axis, up))  13.3 us
    unnamed x24, local copies, waits for them, and re-layouts  5.8 us
  transfers between devices with their start and end apart: 10, of which 7 were waited for; matrix products, arithmetic and copies ran while one was open for 4% of the time, Pallas kernels for 0%

profile of v1, /device:TPU:0, one launch (start us, length us, event | category | flops | bytes accessed | tf_op | source)
XLA Modules:
  0.0 262.2 jit_solution(12004227245258094636)
XLA Ops:
  7.2 0.0 reduce-scatter.3.cloned.1.call-start
  7.2 3.0 %collective-permute-start = (bf16[16,4608]{1,0:T(8,128)(2,1)}, bf16[16,4608]{1,0:T(8,128)(2,1)S(1)}, u32[]{:S(2)}, u32[]{:S(2)}) collective-permute-start(bf16[16,4608]{1,0:T(8,128)(2,1)} %param.6), channel_id=1, source_target_pairs={{0,4},{4,8},{8,12},{12,16},{16,20},{20,24},{24,28},{28,0},{1,5},{5... | collective-permute-start | bytes 442376 | tf_op jit(solution)/shard_map/ppermute | solution.py:14
  10.2 7.1 %collective-permute-done = bf16[16,4608]{1,0:T(8,128)(2,1)S(1)} collective-permute-done((bf16[16,4608]{1,0:T(8,128)(2,1)}, bf16[16,4608]{1,0:T(8,128)(2,1)S(1)}, u32[]{:S(2)}, u32[]{:S(2)}) %collective-permute-start) | collective-permute-done | bytes 147488 | tf_op jit(solution)/shard_map/ppermute | solution.py:14
  17.3 0.0 collective-permute-start.1
  17.3 4.7 %collective-permute-start.4 = (bf16[16,4608]{1,0:T(8,128)(2,1)}, bf16[16,4608]{1,0:T(8,128)(2,1)S(1)}, u32[]{:S(2)}, u32[]{:S(2)}) collective-permute-start(bf16[16,4608]{1,0:T(8,128)(2,1)} %param.6), channel_id=1, source_target_pairs={{0,28},{4,0},{8,4},{12,8},{16,12},{20,16},{24,20},{28,24},{1,29},{... | collective-permute-start | bytes 442376 | tf_op jit(solution)/shard_map/ppermute | solution.py:16
  22.1 3.2 %collective-permute-done.1 = bf16[16,4608]{1,0:T(8,128)(2,1)S(1)} collective-permute-done((bf16[16,4608]{1,0:T(8,128)(2,1)S(1)}, bf16[16,4608]{1,0:T(8,128)(2,1)S(1)}, u32[]{:S(2)}, u32[]{:S(2)}) %collective-permute-start.1) | collective-permute-done | bytes 147488 | tf_op jit(solution)/shard_map/ppermute | solution.py:14
  25.2 0.6 collective-permute-start.2
  25.8 0.0 collective-permute-done.4
  25.8 4.3 %collective-permute-start.5 = (bf16[16,4608]{1,0:T(8,128)(2,1)S(1)}, bf16[16,4608]{1,0:T(8,128)(2,1)S(1)}, u32[]{:S(2)}, u32[]{:S(2)}) collective-permute-start(bf16[16,4608]{1,0:T(8,128)(2,1)S(1)} %collective-permute-done.4), channel_id=1, source_target_pairs={{0,28},{4,0},{8,4},{12,8},{16,12},{20,16},{24,20},{28,24},{1,29},{... | collective-permute-start | bytes 442376 | tf_op jit(solution)/shard_map/ppermute | solution.py:16
  30.2 3.0 %collective-permute-done.2 = bf16[16,4608]{1,0:T(8,128)(2,1)S(1)} collective-permute-done((bf16[16,4608]{1,0:T(8,128)(2,1)S(1)}, bf16[16,4608]{1,0:T(8,128)(2,1)S(1)}, u32[]{:S(2)}, u32[]{:S(2)}) %collective-permute-start.2) | collective-permute-done | bytes 147488 | tf_op jit(solution)/shard_map/ppermute | solution.py:14
  33.2 0.0 collective-permute-start.3
  33.2 1.2 dynamic-slice
  35.1 0.9 dynamic-update-slice
  35.9 21.8 %all-reduce = bf16[128]{0:T(256)(128)(2,1)S(1)} all-reduce(bf16[128]{0:T(256)(128)(2,1)S(1)} %dynamic-update-slice), channel_id=1, replica_groups=mesh['dp'=8,'tensor'=4] {'dp'}, use_global_device_ids=true, to_apply=%add | all-reduce | flops 128 | bytes 512
  57.8 0.9 dynamic-update-slice.2
  58.6 0.8 dynamic-update-slice.1
  59.5 6.8 %all-reduce.3 = (s32[128]{0:T(128)S(1)}, s32[128]{0:T(128)S(1)}) all-reduce(s32[128]{0:T(128)S(1)} %dynamic-update-slice.2, s32[128]{0:T(128)S(1)} %dynamic-update-slice.1), channel_id=1, replica_groups=mesh['dp'=8,'tensor'=4] {'dp'}, use_global_device_ids=true, to_apply=%add.2 | all-reduce | flops 256 | bytes 2048
  66.2 0.0 copy-start
  66.3 0.0 collective-permute-done.5
  66.3 4.6 %collective-permute-start.6 = (bf16[16,4608]{1,0:T(8,128)(2,1)S(1)}, bf16[16,4608]{1,0:T(8,128)(2,1)S(1)}, u32[]{:S(2)}, u32[]{:S(2)}) collective-permute-start(bf16[16,4608]{1,0:T(8,128)(2,1)S(1)} %collective-permute-done.5), channel_id=1, source_target_pairs={{0,28},{4,0},{8,4},{12,8},{16,12},{20,16},{24,20},{28,24},{1,29},{... | collective-permute-start | bytes 442376 | tf_op jit(solution)/shard_map/ppermute | solution.py:16
  70.8 0.0 collective-permute-done.3
  70.9 0.9 constant_dynamic-update-slice_fusion.11
  71.9 1.6 collective-permute-done.6
  73.6 0.9 constant_dynamic-update-slice_fusion.3
  74.6 0.0 copy-done
  74.6 1.7 fusion.3
  76.3 40.6 %psum.7 = f32[128]{0:T(128)S(1)} all-reduce(f32[128]{0:T(128)S(1)} %get-tuple-element.4), channel_id=1, replica_groups=mesh['dp'=8,'tensor'=4] {'dp','tensor'}, use_global_device_ids=true, to_apply=%region_1.2 | all-reduce | flops 128 | bytes 1024 | tf_op jit(solution)/shard_map/psum | solution.py:42
  116.9 4.6 %fusion.10 = f32[128,4608]{1,0:T(8,128)} fusion(bf16[512,4608]{1,0:T(8,128)(2,1)} %param.7, f32[128,512]{1,0:T(8,128)S(1)} %get-tuple-element.5, s32[512]{0:T(512)S(1)} %iota_add_fusion, f32[128]{0:T(128)S(1)} %psum.7, f32[128]{0:T(128)S(1)} %convert_element_type.13, s32[128]{0:T(128)S(1)} %get-tuple-element.3), kind=kOutput, calls=%fused_computation.31 | convolution fusion | flops 604635136 | bytes 7343616 | tf_op jit(solution)/shard_map/dot_general | solution.py:49
  121.5 0.0 reduce-scatter.3.cloned.1.call-update
  121.5 0.0 all-gather.2.cloned.1.call-start
  121.6 0.7 all-gather.2.cloned.1.call-update
  122.3 0.0 reduce-scatter.5.cloned.1.call-start
  122.3 68.9 %reduce-scatter.3.cloned.1.call-done = f32[16,4608]{1,0:T(8,128)} async-done(((f32[128,4608]{1,0:T(8,128)}), f32[16,4608]{1,0:T(8,128)}) %reduce-scatter.3.cloned.1.call-update) | async-done | bytes 294928 | tf_op jit(solution)/shard_map/reduce_scatter | solution.py:48
  191.2 0.0 reduce-scatter.5.cloned.1.call-update
  191.3 42.3 %all-gather.2.cloned.1.call-done = bf16[128,4608]{1,0:T(8,128)(2,1)} async-done(((bf16[16,4608]{1,0:T(8,128)(2,1)}), bf16[128,4608]{1,0:T(8,128)(2,1)}) %all-gather.2.cloned.1.call-update) | async-done | bytes 1179664 | tf_op jit(solution)/shard_map/all_gather | solution.py:33
  233.5 2.7 %fusion.4 = f32[512,4608]{1,0:T(8,128)S(1)} fusion(bf16[128,4608]{1,0:T(8,128)(2,1)} %all-gather.2.cloned.1.call-done, s32[128]{0:T(128)S(1)} %get-tuple-element.2, s32[512]{0:T(512)S(1)} %iota_add_fusion), kind=kOutput, calls=%fused_computation.8 | convolution fusion | flops 604045312 | bytes 10619392 | tf_op jit(solution)/shard_map/dot_general | solution.py:59
  236.2 3.7 %add_convert_fusion = bf16[512,4608]{1,0:T(8,128)(2,1)} fusion(f32[512,4608]{1,0:T(8,128)S(1)} %fusion.4, bf16[256,4608]{1,0:T(8,128)(2,1)S(1)} %constant_dynamic-update-slice_fusion, s32[]{:T(128)S(6)} %select_n.14, f32[128,512]{1,0:T(8,128)S(1)} %get-tuple-element.5, s32[512]{0:T(512)S(1)} %iota_add_fusion, f32[128]{0:T(128)S(1)} %psum.7, ...), kind=kOutput, calls=%fused_computation | convolution fusion | flops 611713024 | bytes 15601156 | tf_op jit(solution)/shard_map/dot_general | solution.py:55
  240.0 15.7 %reduce-scatter.5.cloned.1.call-done = f32[16,1152]{1,0:T(8,128)} async-done(((f32[16,4608]{1,0:T(8,128)}), f32[16,1152]{1,0:T(8,128)}) %reduce-scatter.5.cloned.1.call-update) | async-done | bytes 73744 | tf_op jit(solution)/shard_map/reduce_scatter | solution.py:54
  (19 shorter events, 0.2 us)
Async XLA Ops:
  7.2 184.1 %reduce-scatter.3.cloned.1.call-start = ((), (), s32[]{:S(2)}) async-start(), calls=%async_computation.3 | async-start | bytes 2654208 | tf_op jit(solution)/shard_map/reduce_scatter | solution.py:48
  7.2 10.1 %collective-permute-start = (bf16[16,4608]{1,0:T(8,128)(2,1)}, bf16[16,4608]{1,0:T(8,128)(2,1)S(1)}, u32[]{:S(2)}, u32[]{:S(2)}) collective-permute-start(bf16[16,4608]{1,0:T(8,128)(2,1)} %param.6), channel_id=1, source_target_pairs={{0,4},{4,8},{8,12},{12,16},{16,20},{20,24},{24,28},{28,0},{1,5},{5... | collective-permute-start | bytes 442376 | tf_op jit(solution)/shard_map/ppermute | solution.py:14
  17.3 7.9 %collective-permute-start.1 = (bf16[16,4608]{1,0:T(8,128)(2,1)S(1)}, bf16[16,4608]{1,0:T(8,128)(2,1)S(1)}, u32[]{:S(2)}, u32[]{:S(2)}) collective-permute-start(bf16[16,4608]{1,0:T(8,128)(2,1)S(1)} %collective-permute-done), channel_id=1, source_target_pairs={{0,4},{4,8},{8,12},{12,16},{16,20},{20,24},{24,28},{28,0},{1,5},{5... | collective-permute-start | bytes 442376 | tf_op jit(solution)/shard_map/ppermute | solution.py:14
  17.3 8.5 %collective-permute-start.4 = (bf16[16,4608]{1,0:T(8,128)(2,1)}, bf16[16,4608]{1,0:T(8,128)(2,1)S(1)}, u32[]{:S(2)}, u32[]{:S(2)}) collective-permute-start(bf16[16,4608]{1,0:T(8,128)(2,1)} %param.6), channel_id=1, source_target_pairs={{0,28},{4,0},{8,4},{12,8},{16,12},{20,16},{24,20},{28,24},{1,29},{... | collective-permute-start | bytes 442376 | tf_op jit(solution)/shard_map/ppermute | solution.py:16
  25.2 7.9 %collective-permute-start.2 = (bf16[16,4608]{1,0:T(8,128)(2,1)S(1)}, bf16[16,4608]{1,0:T(8,128)(2,1)S(1)}, u32[]{:S(2)}, u32[]{:S(2)}) collective-permute-start(bf16[16,4608]{1,0:T(8,128)(2,1)S(1)} %collective-permute-done.1), channel_id=1, source_target_pairs={{0,4},{4,8},{8,12},{12,16},{16,20},{20,24},{24,28},{28,0},{1,5},{5... | collective-permute-start | bytes 442376 | tf_op jit(solution)/shard_map/ppermute | solution.py:14
  25.8 40.4 %collective-permute-start.5 = (bf16[16,4608]{1,0:T(8,128)(2,1)S(1)}, bf16[16,4608]{1,0:T(8,128)(2,1)S(1)}, u32[]{:S(2)}, u32[]{:S(2)}) collective-permute-start(bf16[16,4608]{1,0:T(8,128)(2,1)S(1)} %collective-permute-done.4), channel_id=1, source_target_pairs={{0,28},{4,0},{8,4},{12,8},{16,12},{20,16},{24,20},{28,24},{1,29},{... | collective-permute-start | bytes 442376 | tf_op jit(solution)/shard_map/ppermute | solution.py:16
  33.2 37.7 %collective-permute-start.3 = (bf16[16,4608]{1,0:T(8,128)(2,1)S(1)}, bf16[16,4608]{1,0:T(8,128)(2,1)S(1)}, u32[]{:S(2)}, u32[]{:S(2)}) collective-permute-start(bf16[16,4608]{1,0:T(8,128)(2,1)S(1)} %collective-permute-done.2), channel_id=1, source_target_pairs={{0,4},{4,8},{8,12},{12,16},{16,20},{20,24},{24,28},{28,0},{1,5},{5... | collective-permute-start | bytes 442376 | tf_op jit(solution)/shard_map/ppermute | solution.py:14
  66.2 8.3 %copy-start = (bf16[512,4608]{1,0:T(8,128)(2,1)S(1)}, bf16[512,4608]{1,0:T(8,128)(2,1)}, u32[]{:S(2)}) copy-start(bf16[512,4608]{1,0:T(8,128)(2,1)} %param.7) | copy-start | bytes 14155780
  66.3 7.2 %collective-permute-start.6 = (bf16[16,4608]{1,0:T(8,128)(2,1)S(1)}, bf16[16,4608]{1,0:T(8,128)(2,1)S(1)}, u32[]{:S(2)}, u32[]{:S(2)}) collective-permute-start(bf16[16,4608]{1,0:T(8,128)(2,1)S(1)} %collective-permute-done.5), channel_id=1, source_target_pairs={{0,28},{4,0},{8,4},{12,8},{16,12},{20,16},{24,20},{28,24},{1,29},{... | collective-permute-start | bytes 442376 | tf_op jit(solution)/shard_map/ppermute | solution.py:16
  121.5 112.0 %all-gather.2.cloned.1.call-start = ((), (), s32[]{:S(2)}) async-start(), calls=%async_computation.2 | async-start | bytes 1327104 | tf_op jit(solution)/shard_map/all_gather | solution.py:33
  122.3 133.4 %reduce-scatter.5.cloned.1.call-start = ((), (), s32[]{:S(2)}) async-start(), calls=%async_computation.4 | async-start | bytes 368640 | tf_op jit(solution)/shard_map/reduce_scatter | solution.py:54
Sparse Core Ops, SparseCore 0:
  121.7 69.5 reduce-scatter.2
  193.4 40.0 all-gather.1
  236.6 19.0 reduce-scatter.4
